TPU v7x, 512 devices: a whole 4x4x16 slice. The times are simulated.
512 devices in a mesh: gx: 16 (over x, y_lo, core), gy: 32 (over y_hi, z).
Axes of the slice: x: 4, y: 4 (y_hi: 2, y_lo: 2; y = y_hi * 2 + y_lo), z: 16, core: 2. Of those that a mesh axis runs over, the one named last changes fastest.
Arguments:
- plate_motion: bfloat16 [32, 64, 128, 2, 128], P('gx', 'gy'), may hold values from -6 to 6
- adjoint_load: bfloat16 [32, 64, 128, 2, 128], P('gx', 'gy'), may hold values from -6 to 6
- excitation: bfloat16 [32, 64, 128, 2, 128], P('gx', 'gy'), may hold values from -6 to 6
- coupling: bfloat16 [32, 64, 5, 2, 128, 128], P('gx', 'gy'), may hold values from -0.25 to 0.25
- joints: int32 [32, 64, 4], P('gx', 'gy'), may hold values 0 or 1
- hydro: bfloat16 [2, 16384, 16384], P(None, 'gx', 'gy'), may hold values from -0.046875 to 0.046875
- panel_map: bfloat16 [16384, 2, 2, 128], P(('gx', 'gy')), may hold values from -0.25 to 0.25
Outputs:
- residual: float32 [32, 64, 128, 2, 128], P('gx', 'gy')
- multiplier: float32 [32, 64, 128, 2, 128], P('gx', 'gy')
- sensitivity: float32 [32, 64], P('gx', 'gy')
All inputs are finite; a program needn't handle non-finite values. No bound on the sum of `joints` on one device may be relied on, other than what follows from the above.
Results may differ from a plain program's by a relative error of at most 0.0031.
Values may be sent and summed in bfloat16 or wider, within the bound.
A program may use at most 64 MiB of HBM per device.

v0:
```python
import math
import jax
import jax.numpy as jnp
from jax import lax
from jax.sharding import PartitionSpec as P


def extended(x, sides, width):
    for axis, dim in sides:
        size, length = (lax.axis_size(axis), x.shape[dim])
        up = [(i, (i + 1) % size) for i in range(size - 1)]
        down = [(j, i) for i, j in up]
        last = lax.slice_in_dim(x, length - width, length, axis=dim)
        first = lax.slice_in_dim(x, 0, width, axis=dim)
        before = lax.ppermute(last, axis, up)
        after = lax.ppermute(first, axis, down)
        x = jnp.concatenate([before, x, after], axis=dim)
    return x


def complex_apply(form, coupling, vector):
    real_c = coupling[..., 0, :, :]
    imag_c = coupling[..., 1, :, :]
    real_v = vector[..., 0, :]
    imag_v = vector[..., 1, :]

    def mult(matrix, values):
        return jnp.einsum(form, matrix, values, preferred_element_type=jnp.float32)

    return jnp.stack(
        [mult(real_c, real_v) - mult(imag_c, imag_v), mult(real_c, imag_v) + mult(imag_c, real_v)],
        axis=-2,
    )


def adjoint_apply(form, coupling, vector):
    real_c = coupling[..., 0, :, :]
    imag_c = coupling[..., 1, :, :]
    real_v = vector[..., 0, :]
    imag_v = vector[..., 1, :]

    def mult(matrix, values):
        return jnp.einsum(form, matrix, values, preferred_element_type=jnp.float32)

    return jnp.stack(
        [mult(real_c, real_v) + mult(imag_c, imag_v), mult(real_c, imag_v) - mult(imag_c, real_v)],
        axis=-2,
    )


def plain_product(matrix, values):
    return jnp.dot(matrix, values, preferred_element_type=jnp.float32)


def flipped_product(matrix, values):
    return lax.dot_general(
        matrix, values, (((0,), (0,)), ((), ())), preferred_element_type=jnp.float32
    )


def on_device(plate_motion, adjoint_load, excitation, coupling, joints, hydro, panel_map):
    rows_count = plate_motion.shape[0]
    cols_count = plate_motion.shape[1]
    panel_count = panel_map.shape[0]
    unknowns = plate_motion.shape[4]
    cases = plate_motion.shape[2]
    links = joints.astype(jnp.float32)[:, :, :, None, None, None]
    padded = extended(plate_motion, (("gx", 0), ("gy", 1)), 1)
    beside_all = jnp.stack(
        [
            padded[0:rows_count, 1:-1],
            padded[2:, 1:-1],
            padded[1:-1, 0:cols_count],
            padded[1:-1, 2:],
        ],
        axis=2,
    )
    own = complex_apply("xyij,xyhj->xyhi", coupling[:, :, 0], plate_motion)
    structural = own + jnp.sum(
        links * complex_apply("xydij,xydhj->xydhi", coupling[:, :, 1:], beside_all), axis=2
    )
    outgoing = links * adjoint_apply("xydji,xyhj->xydhi", coupling[:, :, 1:], adjoint_load)
    own_adjoint = adjoint_apply("xyji,xyhj->xyhi", coupling[:, :, 0], adjoint_load)
    layered = extended(outgoing, (("gx", 0), ("gy", 1)), 1)
    incoming = (
        layered[2:, 1:-1, 0] + layered[:-2, 1:-1, 1] + layered[1:-1, 2:, 2] + layered[1:-1, :-2, 3]
    )
    lift = math.sqrt(rows_count * cols_count * unknowns / panel_count)
    motion_panels = jnp.einsum(
        "nxyk,xyhck->cnh", panel_map, plate_motion, preferred_element_type=jnp.float32
    ).astype(jnp.bfloat16)
    load_panels = jnp.einsum(
        "nxyk,xyhck->cnh", panel_map, adjoint_load, preferred_element_type=jnp.float32
    ).astype(jnp.bfloat16)
    piece = lax.all_gather(motion_panels, "gx", axis=1, tiled=True)
    first = plain_product(hydro[0], piece[0]) - plain_product(hydro[1], piece[1])
    second = plain_product(hydro[0], piece[1]) + plain_product(hydro[1], piece[0])
    pressure_part = jnp.stack([first, second])
    piece = lax.all_gather(load_panels, "gy", axis=1, tiled=True)
    first = flipped_product(hydro[0], piece[0]) + flipped_product(hydro[1], piece[1])
    second = flipped_product(hydro[0], piece[1]) - flipped_product(hydro[1], piece[0])
    reaction_part = jnp.stack([first, second])
    pressure_band = lax.psum(pressure_part, "gy")
    pressure = lax.dynamic_slice_in_dim(
        pressure_band, lax.axis_index("gy") * panel_count, panel_count, 1
    )
    reaction_band = lax.psum(reaction_part, "gx")
    reaction = lax.dynamic_slice_in_dim(
        reaction_band, lax.axis_index("gx") * panel_count, panel_count, 1
    )
    pressure = pressure.astype(jnp.bfloat16)
    reaction = reaction.astype(jnp.bfloat16)
    pressure_force = jnp.einsum(
        "nxyk,cnh->xyhck", panel_map, pressure, preferred_element_type=jnp.float32
    )
    reaction_force = jnp.einsum(
        "nxyk,cnh->xyhck", panel_map, reaction, preferred_element_type=jnp.float32
    )
    residual = structural + lift * pressure_force - excitation.astype(jnp.float32)
    multiplier = own_adjoint + incoming + lift * reaction_force
    sensitivity = jnp.sum(multiplier * own, axis=(2, 3, 4)) / math.sqrt(cases * unknowns)
    return (residual, multiplier, sensitivity)


def solution(mesh):
    placed = (
        P("gx", "gy", None, None, None),
        P("gx", "gy", None, None, None),
        P("gx", "gy", None, None, None),
        P("gx", "gy", None, None, None, None),
        P("gx", "gy", None),
        P(None, "gx", "gy"),
        P(("gx", "gy"), None, None, None),
    )
    return jax.shard_map(
        on_device,
        mesh=mesh,
        in_specs=placed,
        out_specs=(P("gx", "gy", None, None, None), P("gx", "gy", None, None, None), P("gx", "gy")),
        check_vma=False,
    )
```

profile of v0, /device:TPU:14, one launch (start us, length us, event | category | flops | bytes accessed | tf_op | source)
XLA Modules:
  0.0 440.0 jit_solution(6919222201309677431)
XLA Ops:
  0.6 1.0 copy.43
  1.7 0.7 fusion.106
  2.4 1.9 collective-permute-start
  4.3 3.6 collective-permute-start.1
  8.0 1.3 slice_bitcast_fusion.2
  9.4 1.3 fusion.59
  10.9 1.0 copy_bitcast_fusion
  12.1 84.5 %all_gather.7 = bf16[2,1024,128]{2,1,0:T(8,128)(2,1)S(1)} all-gather(bf16[2,32,128]{2,1,0:T(8,128)(2,1)S(1)} %fusion.19), channel_id=1, replica_groups=mesh['gx'=16,'gy'=32] {'gy'}, dimensions={1}, use_global_device_ids=true | all-gather | bytes 540672 | tf_op jit(solution)/shard_map/all_gather | solution.py:99
  96.6 1.2 fusion.25
  97.9 1.2 fusion.27
  99.3 16.8 %all_gather.6 = bf16[2,512,128]{2,1,0:T(8,128)(2,1)S(1)} all-gather(bf16[2,32,128]{2,1,0:T(8,128)(2,1)S(1)} %fusion.20), channel_id=1, replica_groups=mesh['gx'=16,'gy'=32] {'gx'}, dimensions={1}, use_global_device_ids=true | all-gather | bytes 278528 | tf_op jit(solution)/shard_map/all_gather | solution.py:95
  116.2 1.2 fusion.29
  117.4 1.2 fusion.31
  118.9 2.0 fusion.15
  120.9 1.6 fusion.16
  122.6 0.4 fusion.5
  123.0 0.4 fusion.6
  123.5 0.3 copy-done
  124.4 0.6 copy-done.5
  125.1 0.9 constant_dynamic-update-slice_fusion
  126.1 1.3 collective-permute-start.2
  127.4 1.3 collective-permute-start.3
  128.7 1.1 pad_maximum_fusion.2
  129.9 0.9 fusion.66
  130.8 2.9 collective-permute-done.2
  133.7 4.1 collective-permute-done.3
  138.1 0.5 fusion.51
  138.6 0.5 fusion.47
  139.1 0.5 fusion.4
  139.6 0.5 fusion.3
  140.1 1.3 maximum_multiply_fusion.1
  141.3 1.6 fusion.104
  142.9 1.9 collective-permute-start.4
  144.8 3.4 collective-permute-start.5
  148.2 0.8 pad_maximum_fusion.12
  149.4 0.9 fusion.12
  150.7 18.0 %collective-permute-done.4 = f32[1,2,4,128,2,128]{5,3,1,0,4,2:T(8,128)} collective-permute-done((f32[1,2,4,128,2,128]{5,3,1,0,4,2:T(8,128)}, f32[1,2,4,128,2,128]{5,3,1,0,4,2:T(8,128)}, u32[]{:S(2)}, u32[]{:S(2)}) %collective-permute-start.4) | collective-permute-done | bytes 1048608 | tf_op jit(solution)/shard_map/ppermute | solution.py:16
  168.7 2.0 pad_maximum_fusion
  170.7 2.5 fusion.103
  173.2 1.4 collective-permute-start.6
  174.6 5.9 %collective-permute-start.7 = (f32[4,1,4,128,2,128]{5,3,1,0,4,2:T(8,128)}, f32[4,1,4,128,2,128]{5,3,1,0,4,2:T(8,128)}, u32[]{:S(2)}, u32[]{:S(2)}) collective-permute-start(f32[4,1,4,128,2,128]{5,3,1,0,4,2:T(8,128)} %get-tuple-element.10), channel_id=1, source_target_pairs={{0,1},{1,2},{2,3},{3,4},{4,5},{5,6},{6,7},{7,8},{8,9},{9,10},{10,1... | collective-permute-start | bytes 6291464 | tf_op jit(solution)/shard_map/ppermute | solution.py:15
  181.0 98.1 %all-reduce.2 = bf16[2,512,128]{2,1,0:T(8,128)(2,1)} all-reduce(f32[2,512,128]{2,1,0:T(8,128)} %pad_maximum_fusion.12), channel_id=1, replica_groups=mesh['gx'=16,'gy'=32] {'gx'}, use_global_device_ids=true, to_apply=%region_2.0 | all-reduce | flops 131072 | bytes 786432 | tf_op jit(solution)/shard_map/psum | solution.py:107
  279.1 154.9 %all-reduce.3 = bf16[2,1024,128]{2,1,0:T(8,128)(2,1)} all-reduce(f32[2,1024,128]{2,1,0:T(8,128)} %pad_maximum_fusion.2), channel_id=1, replica_groups=mesh['gx'=16,'gy'=32] {'gy'}, use_global_device_ids=true, to_apply=%region_1.0 | all-reduce | flops 262144 | bytes 1572864 | tf_op jit(solution)/shard_map/psum | solution.py:103
  434.0 1.4 fusion.10
  435.4 1.2 copy.80
  436.6 1.6 multiply_reduce_fusion
  438.2 1.2 copy.81
  439.4 0.6 broadcast_multiply_fusion
  (50 shorter events, 3.1 us)
Async XLA Ops:
  0.6 8.6 %copy-start.9 = (bf16[2,2,128,2,128]{4,3,2,1,0:T(2,128)(2,1)S(1)}, bf16[2,2,128,2,128]{4,3,2,1,0:T(2,128)(2,1)}, u32[]{:S(2)}) copy-start(bf16[2,2,128,2,128]{4,3,2,1,0:T(2,128)(2,1)} %param.8) | copy-start | bytes 786436
  2.4 122.0 %collective-permute-start = (bf16[1,2,128,2,128]{4,2,1,0,3:T(8,128)(2,1)}, bf16[1,2,128,2,128]{4,2,1,0,3:T(8,128)(2,1)S(1)}, u32[]{:S(2)}, u32[]{:S(2)}) collective-permute-start(bf16[1,2,128,2,128]{4,2,1,0,3:T(8,128)(2,1)} %get-tuple-element.24), channel_id=1, source_target_pairs={{0,32},{32,64},{64,96},{96,128},{128,160},{160,192},{192,224},{224... | collective-permute-start | bytes 393224 | tf_op jit(solution)/shard_map/ppermute | solution.py:15
  4.3 120.8 %collective-permute-start.1 = (bf16[1,2,128,2,128]{4,2,1,0,3:T(8,128)(2,1)}, bf16[1,2,128,2,128]{4,2,1,0,3:T(8,128)(2,1)}, u32[]{:S(2)}, u32[]{:S(2)}) collective-permute-start(bf16[1,2,128,2,128]{4,2,1,0,3:T(8,128)(2,1)} %get-tuple-element.23), channel_id=1, source_target_pairs={{32,0},{64,32},{96,64},{128,96},{160,128},{192,160},{224,192},{256... | collective-permute-start | bytes 393224 | tf_op jit(solution)/shard_map/ppermute | solution.py:16
  9.3 2.6 copy-start.10
  9.3 87.3 %copy-start.1 = (bf16[2,1024,512]{2,1,0:T(8,128)(2,1)S(1)}, bf16[2,1024,512]{2,1,0:T(8,128)(2,1)}, u32[]{:S(2)}) copy-start(bf16[2,1024,512]{2,1,0:T(8,128)(2,1)} %param.12) | copy-start | bytes 6291460
  12.1 87.0 %copy-start.4 = (bf16[2,2,128,2,128]{4,3,2,1,0:T(2,128)(2,1)S(1)}, bf16[2,2,128,2,128]{4,3,2,1,0:T(2,128)(2,1)}, u32[]{:S(2)}) copy-start(bf16[2,2,128,2,128]{4,3,2,1,0:T(2,128)(2,1)} %param.7) | copy-start | bytes 786436
  96.6 19.5 %copy-start.8 = (bf16[2,1024,128]{2,1,0:T(8,128)(2,1)}, bf16[2,1024,128]{2,1,0:T(8,128)(2,1)S(1)}, u32[]{:S(2)}) copy-start(bf16[2,1024,128]{2,1,0:T(8,128)(2,1)S(1)} %all_gather.7) | copy-start | bytes 1572868
  99.1 19.5 %copy-start.12 = (s32[2,2,4]{2,1,0:T(2,128)S(1)}, s32[2,2,4]{2,1,0:T(2,128)}, u32[]{:S(2)}) copy-start(s32[2,2,4]{2,1,0:T(2,128)} %param.11) | copy-start | bytes 196
  118.7 2.2 copy-start.2
  118.7 3.8 copy-start.7
  120.9 2.1 copy-start.6
  122.6 1.2 copy-start
  124.1 1.0 copy-start.5
  126.1 7.6 %collective-permute-start.2 = (bf16[4,1,128,2,128]{4,2,1,0,3:T(8,128)(2,1)S(1)}, bf16[4,1,128,2,128]{4,2,1,0,3:T(8,128)(2,1)S(1)}, u32[]{:S(2)}, u32[]{:S(2)}) collective-permute-start(bf16[4,1,128,2,128]{4,2,1,0,3:T(8,128)(2,1)S(1)} %get-tuple-element.19), channel_id=1, source_target_pairs={{0,1},{1,2},{2,3},{3,4},{4,5},{5,6},{6,7},{7,8},{8,9},{9,10},{10,1... | collective-permute-start | bytes 786440 | tf_op jit(solution)/shard_map/ppermute | solution.py:15
  127.4 10.4 %collective-permute-start.3 = (bf16[4,1,128,2,128]{4,2,1,0,3:T(8,128)(2,1)S(1)}, bf16[4,1,128,2,128]{4,2,1,0,3:T(8,128)(2,1)S(1)}, u32[]{:S(2)}, u32[]{:S(2)}) collective-permute-start(bf16[4,1,128,2,128]{4,2,1,0,3:T(8,128)(2,1)S(1)} %get-tuple-element.20), channel_id=1, source_target_pairs={{1,0},{2,1},{3,2},{4,3},{5,4},{6,5},{7,6},{8,7},{9,8},{10,9},{11,1... | collective-permute-start | bytes 786440 | tf_op jit(solution)/shard_map/ppermute | solution.py:16
  142.9 25.8 %collective-permute-start.4 = (f32[1,2,4,128,2,128]{5,3,1,0,4,2:T(8,128)}, f32[1,2,4,128,2,128]{5,3,1,0,4,2:T(8,128)}, u32[]{:S(2)}, u32[]{:S(2)}) collective-permute-start(f32[1,2,4,128,2,128]{5,3,1,0,4,2:T(8,128)} %get-tuple-element.12), channel_id=1, source_target_pairs={{32,0},{64,32},{96,64},{128,96},{160,128},{192,160},{224,192},{256... | collective-permute-start | bytes 3145736 | tf_op jit(solution)/shard_map/ppermute | solution.py:16
  144.8 23.8 %collective-permute-start.5 = (f32[1,2,4,128,2,128]{5,3,1,0,4,2:T(8,128)}, f32[1,2,4,128,2,128]{5,3,1,0,4,2:T(8,128)}, u32[]{:S(2)}, u32[]{:S(2)}) collective-permute-start(f32[1,2,4,128,2,128]{5,3,1,0,4,2:T(8,128)} %get-tuple-element.11), channel_id=1, source_target_pairs={{0,32},{32,64},{64,96},{96,128},{128,160},{160,192},{192,224},{224... | collective-permute-start | bytes 3145736 | tf_op jit(solution)/shard_map/ppermute | solution.py:15
  173.2 260.8 %copy-start.11 = (bf16[32,2,2,128]{3,2,1,0:T(2,128)(2,1)S(1)}, bf16[32,2,2,128]{3,2,1,0:T(2,128)(2,1)}, u32[]{:S(2)}) copy-start(bf16[32,2,2,128]{3,2,1,0:T(2,128)(2,1)} %param.13) | copy-start | bytes 98308
  173.2 263.4 %collective-permute-start.6 = (f32[4,1,4,128,2,128]{5,3,1,0,4,2:T(8,128)}, f32[4,1,4,128,2,128]{5,3,1,0,4,2:T(8,128)}, u32[]{:S(2)}, u32[]{:S(2)}) collective-permute-start(f32[4,1,4,128,2,128]{5,3,1,0,4,2:T(8,128)} %get-tuple-element.9), channel_id=1, source_target_pairs={{1,0},{2,1},{3,2},{4,3},{5,4},{6,5},{7,6},{8,7},{9,8},{10,9},{11,1... | collective-permute-start | bytes 6291464 | tf_op jit(solution)/shard_map/ppermute | solution.py:16
  174.6 262.0 %collective-permute-start.7 = (f32[4,1,4,128,2,128]{5,3,1,0,4,2:T(8,128)}, f32[4,1,4,128,2,128]{5,3,1,0,4,2:T(8,128)}, u32[]{:S(2)}, u32[]{:S(2)}) collective-permute-start(f32[4,1,4,128,2,128]{5,3,1,0,4,2:T(8,128)} %get-tuple-element.10), channel_id=1, source_target_pairs={{0,1},{1,2},{2,3},{3,4},{4,5},{5,6},{6,7},{7,8},{8,9},{9,10},{10,1... | collective-permute-start | bytes 6291464 | tf_op jit(solution)/shard_map/ppermute | solution.py:15
  434.0 2.7 copy-start.3
where the time goes:
time: 441 us; the launch traced here: 440 us
  blocking collectives  354 us (80%)
  waiting for transfers between devices  25.1 us (6%)
  starting transfers between devices  20.7 us (5%)
  matrix products  19 us (4%)
  local copies, waits for them, and re-layouts  12.8 us (3%)
  other arithmetic  6.95 us (2%)
    psum x1, blocking collectives, on_device(): pressure_band = lax.psum(pressure_part, 'gy')  155 us
    psum x1, blocking collectives, on_device(): reaction_band = lax.psum(reaction_part, 'gx')  98.1 us
    all_gather x1, blocking collectives, on_device(): piece = lax.all_gather(load_panels, 'gy', axis=1, tiled=True)  84.5 us
    ppermute x4, waiting for transfers between devices, extended(): after = lax.ppermute(first, axis, down)  22.1 us
    all_gather x1, blocking collectives, on_device(): piece = lax.all_gather(motion_panels, 'gx', axis=1, tiled=True)  16.8 us
    ppermute x4, starting transfers between devices, extended(): before = lax.ppermute(last, axis, up)  12.5 us
  transfers between devices with their start and end apart: 8, of which 3 were waited for; matrix products, arithmetic and copies ran while one was open for 5% of the time, Pallas kernels for 0%

commit v1 on v0

--- a/solution.py
+++ b/solution.py
@@ -104,7 +104,7 @@
     pressure = lax.dynamic_slice_in_dim(
         pressure_band, lax.axis_index("gy") * panel_count, panel_count, 1
     )
-    reaction_band = lax.psum(reaction_part, "gx")
+    reaction_band = jnp.sum(lax.all_gather(reaction_part, "gx"), axis=0)
     reaction = lax.dynamic_slice_in_dim(
         reaction_band, lax.axis_index("gx") * panel_count, panel_count, 1
     )

time: 441 us -> 427 us (0.968)
  the two profiles are of different devices: /device:TPU:14 before, /device:TPU:8 now
where the time goes in v1:
time: 427 us
  blocking collectives  276 us (65%)
  waiting for transfers between devices  83.9 us (20%)
  starting transfers between devices  20.1 us (5%)
  between operations  14.5 us (3%)
  matrix products  14 us (3%)
  local copies, waits for them, and re-layouts  10.1 us (2%)
  other arithmetic  8.06 us (2%)
    psum x1, blocking collectives, on_device(): pressure_band = lax.psum(pressure_part, 'gy')  173 us
    all_gather x1, blocking collectives, on_device(): piece = lax.all_gather(load_panels, 'gy', axis=1, tiled=True)  84.4 us
    ppermute x4, waiting for transfers between devices, extended(): before = lax.ppermute(last, axis, up)  79.8 us
    all_gather x1, blocking collectives, on_device(): piece = lax.all_gather(motion_panels, 'gx', axis=1, tiled=True)  18.7 us
    ppermute x4, starting transfers between devices, extended(): before = lax.ppermute(last, axis, up)  11.7 us
  transfers between devices with their start and end apart: 9, of which 3 were waited for; matrix products, arithmetic and copies ran while one was open for 5% of the time, Pallas kernels for 0%

profile of v1, /device:TPU:8, one launch (start us, length us, event | category | flops | bytes accessed | tf_op | source)
XLA Modules:
  0.0 426.9 jit_solution(14185194893389493817)
XLA Ops:
  7.2 1.3 fusion.19
  8.5 84.4 %all_gather.13 = bf16[2,1024,128]{2,1,0:T(8,128)(2,1)S(1)} all-gather(bf16[2,32,128]{2,1,0:T(8,128)(2,1)S(1)} %fusion.19), channel_id=1, replica_groups=mesh['gx'=16,'gy'=32] {'gy'}, dimensions={1}, use_global_device_ids=true | all-gather | bytes 540672 | tf_op jit(solution)/shard_map/all_gather | solution.py:99
  92.9 1.5 fusion.25
  94.5 0.3 fusion.27
  94.8 0.3 fusion.15
  95.2 0.3 fusion.16
  95.6 1.0 copy.109
  96.7 0.7 fusion.106
  97.4 1.9 collective-permute-start.1
  99.3 2.4 collective-permute-start
  101.7 1.0 copy.101
  103.0 18.7 %all_gather.12 = bf16[2,512,128]{2,1,0:T(8,128)(2,1)S(1)} all-gather(bf16[2,32,128]{2,1,0:T(8,128)(2,1)S(1)} %fusion.20), channel_id=1, replica_groups=mesh['gx'=16,'gy'=32] {'gx'}, dimensions={1}, use_global_device_ids=true | all-gather | bytes 278528 | tf_op jit(solution)/shard_map/all_gather | solution.py:95
  121.7 1.0 copy_bitcast_fusion
  123.0 0.3 fusion.59
  123.3 0.3 fusion.57
  123.5 0.4 fusion.29
  124.0 0.3 fusion.2
  124.5 1.3 collective-permute-start.2
  125.8 1.3 collective-permute-start.3
  127.1 0.3 fusion.1
  127.4 4.7 %collective-permute-done.2 = bf16[4,1,128,2,128]{4,2,1,0,3:T(8,128)(2,1)S(1)} collective-permute-done((bf16[4,1,128,2,128]{4,2,1,0,3:T(8,128)(2,1)S(1)}, bf16[4,1,128,2,128]{4,2,1,0,3:T(8,128)(2,1)S(1)}, u32[]{:S(2)}, u32[]{:S(2)}) %collective-permute-start.2) | collective-permute-done | bytes 262176 | tf_op jit(solution)/shard_map/ppermute | solution.py:15
  132.1 4.1 collective-permute-done.3
  136.5 0.5 fusion.47
  137.0 0.5 fusion.3
  137.5 0.5 fusion.51
  138.0 0.5 fusion.4
  138.5 1.3 maximum_multiply_fusion.1
  139.9 2.1 collective-permute-start.5
  142.0 3.9 collective-permute-start.4
  146.1 0.4 fusion.5
  146.6 0.4 fusion.31
  147.0 0.4 fusion.6
  147.4 1.0 pad_maximum_fusion.2
  148.7 75.1 %collective-permute-done.5 = f32[1,2,4,128,2,128]{5,3,1,0,4,2:T(8,128)S(1)} collective-permute-done((f32[1,2,4,128,2,128]{5,3,1,0,4,2:T(8,128)S(1)}, f32[1,2,4,128,2,128]{5,3,1,0,4,2:T(8,128)S(1)}, u32[]{:S(2)}, u32[]{:S(2)}) %collective-permute-start.5) | collective-permute-done | bytes 1048608 | tf_op jit(solution)/shard_map/ppermute | solution.py:15
  223.7 0.4 pad_maximum_fusion
  224.1 0.6 copy-done.2
  224.7 0.3 copy-done.3
  225.1 2.4 fusion.103
  227.5 1.3 collective-permute-start.6
  228.8 5.9 %collective-permute-start.7 = (f32[4,1,4,128,2,128]{5,3,1,0,4,2:T(8,128)}, f32[4,1,4,128,2,128]{5,3,1,0,4,2:T(8,128)}, u32[]{:S(2)}, u32[]{:S(2)}) collective-permute-start(f32[4,1,4,128,2,128]{5,3,1,0,4,2:T(8,128)} %get-tuple-element.13), channel_id=1, source_target_pairs={{0,1},{1,2},{2,3},{3,4},{4,5},{5,6},{6,7},{7,8},{8,9},{9,10},{10,1... | collective-permute-start | bytes 6291464 | tf_op jit(solution)/shard_map/ppermute | solution.py:15
  235.5 0.9 fusion.11
  236.3 173.1 %all-reduce.1 = bf16[2,1024,128]{2,1,0:T(8,128)(2,1)} all-reduce(f32[2,1024,128]{2,1,0:T(8,128)} %pad_maximum_fusion.2), channel_id=1, replica_groups=mesh['gx'=16,'gy'=32] {'gy'}, use_global_device_ids=true, to_apply=%region_1.0 | all-reduce | flops 262144 | bytes 1572864 | tf_op jit(solution)/shard_map/psum | solution.py:103
  409.4 1.4 fusion.10
  410.8 1.2 copy.113
  412.0 4.5 %reduce_sum.28 = bf16[2,512,128]{2,1,0:T(8,128)(2,1)} reduce(f32[16,2,512,128]{3,2,1,0:T(8,128)} %bitcast.197, f32[]{:T(128)} %constant.4.clone.1), dimensions={0}, to_apply=%region_2.0 | reduce | flops 1966080 | bytes 8650756 | tf_op jit(solution)/shard_map/reduce_sum | solution.py:107
  416.6 1.7 multiply_reduce_fusion
  418.2 0.6 broadcast_multiply_fusion
  418.8 1.2 copy.114
  (44 shorter events, 2.5 us)
Async XLA Ops:
  7.2 87.3 %copy-start = (bf16[2,1024,512]{2,1,0:T(8,128)(2,1)S(1)}, bf16[2,1024,512]{2,1,0:T(8,128)(2,1)}, u32[]{:S(2)}) copy-start(bf16[2,1024,512]{2,1,0:T(8,128)(2,1)} %param.12) | copy-start | bytes 6291460
  7.2 404.8 %all-gather.3.cloned.1.call-start = ((), (), s32[]{:S(2)}) async-start(), calls=%async_computation | async-start | bytes 8912896 | tf_op jit(solution)/shard_map/all_gather | solution.py:107
  95.2 1.4 copy-start.5
  95.5 7.2 %copy-start.7 = (s32[2,2,4]{2,1,0:T(2,128)S(1)}, s32[2,2,4]{2,1,0:T(2,128)}, u32[]{:S(2)}) copy-start(s32[2,2,4]{2,1,0:T(2,128)} %param.11) | copy-start | bytes 196
  95.5 7.3 %copy-start.6 = (bf16[32,2,2,128]{3,2,1,0:T(2,128)(2,1)S(1)}, bf16[32,2,2,128]{3,2,1,0:T(2,128)(2,1)}, u32[]{:S(2)}) copy-start(bf16[32,2,2,128]{3,2,1,0:T(2,128)(2,1)} %param.13) | copy-start | bytes 98308
  97.4 27.0 %collective-permute-start.1 = (bf16[1,2,128,2,128]{4,2,1,0,3:T(8,128)(2,1)}, bf16[1,2,128,2,128]{4,2,1,0,3:T(8,128)(2,1)S(1)}, u32[]{:S(2)}, u32[]{:S(2)}) collective-permute-start(bf16[1,2,128,2,128]{4,2,1,0,3:T(8,128)(2,1)} %get-tuple-element.26), channel_id=1, source_target_pairs={{32,0},{64,32},{96,64},{128,96},{160,128},{192,160},{224,192},{256... | collective-permute-start | bytes 393224 | tf_op jit(solution)/shard_map/ppermute | solution.py:16
  99.3 25.0 %collective-permute-start = (bf16[1,2,128,2,128]{4,2,1,0,3:T(8,128)(2,1)}, bf16[1,2,128,2,128]{4,2,1,0,3:T(8,128)(2,1)S(1)}, u32[]{:S(2)}, u32[]{:S(2)}) collective-permute-start(bf16[1,2,128,2,128]{4,2,1,0,3:T(8,128)(2,1)} %get-tuple-element.27), channel_id=1, source_target_pairs={{0,32},{32,64},{64,96},{96,128},{128,160},{160,192},{192,224},{224... | collective-permute-start | bytes 393224 | tf_op jit(solution)/shard_map/ppermute | solution.py:15
  102.8 20.0 %copy-start.4 = (bf16[2,2,5,2,128,128]{5,4,3,2,1,0:T(8,128)(2,1)S(1)}, bf16[2,2,5,2,128,128]{5,4,3,2,1,0:T(8,128)(2,1)}, u32[]{:S(2)}) copy-start(bf16[2,2,5,2,128,128]{5,4,3,2,1,0:T(8,128)(2,1)} %param.10) | copy-start | bytes 3932164
  124.5 7.6 %collective-permute-start.2 = (bf16[4,1,128,2,128]{4,2,1,0,3:T(8,128)(2,1)S(1)}, bf16[4,1,128,2,128]{4,2,1,0,3:T(8,128)(2,1)S(1)}, u32[]{:S(2)}, u32[]{:S(2)}) collective-permute-start(bf16[4,1,128,2,128]{4,2,1,0,3:T(8,128)(2,1)S(1)} %get-tuple-element.22), channel_id=1, source_target_pairs={{0,1},{1,2},{2,3},{3,4},{4,5},{5,6},{6,7},{7,8},{8,9},{9,10},{10,1... | collective-permute-start | bytes 786440 | tf_op jit(solution)/shard_map/ppermute | solution.py:15
  125.8 10.5 %collective-permute-start.3 = (bf16[4,1,128,2,128]{4,2,1,0,3:T(8,128)(2,1)S(1)}, bf16[4,1,128,2,128]{4,2,1,0,3:T(8,128)(2,1)S(1)}, u32[]{:S(2)}, u32[]{:S(2)}) collective-permute-start(bf16[4,1,128,2,128]{4,2,1,0,3:T(8,128)(2,1)S(1)} %get-tuple-element.23), channel_id=1, source_target_pairs={{1,0},{2,1},{3,2},{4,3},{5,4},{6,5},{7,6},{8,7},{9,8},{10,9},{11,1... | collective-permute-start | bytes 786440 | tf_op jit(solution)/shard_map/ppermute | solution.py:16
  139.8 6.3 %copy-start.1 = (bf16[2,1024,512]{2,1,0:T(8,128)(2,1)S(1)}, bf16[2,1024,512]{2,1,0:T(8,128)(2,1)}, u32[]{:S(2)}) copy-start(bf16[2,1024,512]{2,1,0:T(8,128)(2,1)} %param.12) | copy-start | bytes 6291460
  139.9 83.8 %collective-permute-start.5 = (f32[1,2,4,128,2,128]{5,3,1,0,4,2:T(8,128)S(1)}, f32[1,2,4,128,2,128]{5,3,1,0,4,2:T(8,128)S(1)}, u32[]{:S(2)}, u32[]{:S(2)}) collective-permute-start(f32[1,2,4,128,2,128]{5,3,1,0,4,2:T(8,128)S(1)} %get-tuple-element.14), channel_id=1, source_target_pairs={{0,32},{32,64},{64,96},{96,128},{128,160},{160,192},{192,224},{224... | collective-permute-start | bytes 3145736 | tf_op jit(solution)/shard_map/ppermute | solution.py:15
  142.0 81.8 %collective-permute-start.4 = (f32[1,2,4,128,2,128]{5,3,1,0,4,2:T(8,128)S(1)}, f32[1,2,4,128,2,128]{5,3,1,0,4,2:T(8,128)S(1)}, u32[]{:S(2)}, u32[]{:S(2)}) collective-permute-start(f32[1,2,4,128,2,128]{5,3,1,0,4,2:T(8,128)S(1)} %get-tuple-element.15), channel_id=1, source_target_pairs={{32,0},{64,32},{96,64},{128,96},{160,128},{192,160},{224,192},{256... | collective-permute-start | bytes 3145736 | tf_op jit(solution)/shard_map/ppermute | solution.py:16
  223.7 1.0 copy-start.2
  223.7 1.3 copy-start.3
  227.5 189.1 %collective-permute-start.6 = (f32[4,1,4,128,2,128]{5,3,1,0,4,2:T(8,128)}, f32[4,1,4,128,2,128]{5,3,1,0,4,2:T(8,128)}, u32[]{:S(2)}, u32[]{:S(2)}) collective-permute-start(f32[4,1,4,128,2,128]{5,3,1,0,4,2:T(8,128)} %get-tuple-element.12), channel_id=1, source_target_pairs={{1,0},{2,1},{3,2},{4,3},{5,4},{6,5},{7,6},{8,7},{9,8},{10,9},{11,1... | collective-permute-start | bytes 6291464 | tf_op jit(solution)/shard_map/ppermute | solution.py:16
  228.8 187.8 %collective-permute-start.7 = (f32[4,1,4,128,2,128]{5,3,1,0,4,2:T(8,128)}, f32[4,1,4,128,2,128]{5,3,1,0,4,2:T(8,128)}, u32[]{:S(2)}, u32[]{:S(2)}) collective-permute-start(f32[4,1,4,128,2,128]{5,3,1,0,4,2:T(8,128)} %get-tuple-element.13), channel_id=1, source_target_pairs={{0,1},{1,2},{2,3},{3,4},{4,5},{5,6},{6,7},{7,8},{8,9},{9,10},{10,1... | collective-permute-start | bytes 6291464 | tf_op jit(solution)/shard_map/ppermute | solution.py:15
Sparse Core Ops, SparseCore 0:
  96.7 74.0 all-gather.2
